TPU v7x, 32 devices: a whole 2x2x4 slice. The times are simulated.
32 devices in a mesh: dp: 8 (over z, core), expert: 4 (over y, x).
Axes of the slice: x: 2, y: 2, z: 4, core: 2. Of those that a mesh axis runs over, the one named last changes fastest.
Arguments:
- tokens: bfloat16 [24576, 2048], P(('dp', 'expert')), may hold values from -6 to 6
- target: bfloat16 [24576, 2048], P(('dp', 'expert')), may hold values from -4 to 4
- route_index: int32 [8, 4, 4, 16], P('dp', None, 'expert'), may hold values from 0 to 767, as said below
- route_count: int32 [8, 4, 4], P('dp', None, 'expert'), may hold values from 1 to 16, as said below
- route_gate: float32 [8, 4, 4, 16], P('dp', None, 'expert'), may hold values from 0.1 to 1
- gate_weight: bfloat16 [2048, 4, 768], P('dp', 'expert'), may hold values from -0.125 to 0.125
- up_weight: bfloat16 [2048, 4, 768], P('dp', 'expert'), may hold values from -0.125 to 0.125
- down_weight: bfloat16 [2048, 4, 768], P('dp', 'expert'), may hold values from -0.21875 to 0.21875
Outputs:
- token_grad: bfloat16 [24576, 2048], P(('dp', 'expert'))
- gate_gradient: float32 [2048, 4, 768], P('dp', 'expert')
- up_gradient: float32 [2048, 4, 768], P('dp', 'expert')
- down_gradient: float32 [2048, 4, 768], P('dp', 'expert')
Inputs may be any that keep to these rules, and one draw needn't show every extreme that they name: `route_index`: within each list of 16 slots the indices are distinct; each names a token of the source device. `route_count`: in every group one expert has all 16 slots live from every source device; slots at or beyond the count are unused.
All inputs are finite; a program needn't handle non-finite values.
Results may differ from a plain program's by a relative error of at most 0.0059.
Values may be sent and summed in bfloat16 or wider, within the bound.
A program may use at most 128 MiB of HBM per device.

v0:
```python
import jax
import jax.numpy as jnp
from jax import lax
from jax.sharding import PartitionSpec as P


def to_owners(block):
    return lax.all_to_all(block, "expert", split_axis=0, concat_axis=1, tiled=True)


def to_sources(block):
    return lax.all_to_all(block, "expert", split_axis=1, concat_axis=0, tiled=True)


def on_device(
    tokens, target, route_index, route_count, route_gate, gate_weight, up_weight, down_weight
):
    groups = lax.axis_size("dp")
    sources = lax.axis_size("expert")
    local_index = route_index[0, :, 0, :]
    live_count = route_count[0, :, 0]
    per_source = local_index.shape[1]
    model_width = tokens.shape[1]
    usable = jnp.arange(per_source, dtype=jnp.int32)[None, :] < live_count[:, None]
    slot_weight = jnp.where(usable, route_gate[0, :, 0, :], 0.0)
    outgoing = tokens[local_index] * usable[:, :, None].astype(tokens.dtype)
    expert_rows = to_owners(outgoing)
    full_gate, full_up, full_down = (
        lax.all_gather(gate_weight, "dp", axis=0, tiled=True),
        lax.all_gather(up_weight, "dp", axis=0, tiled=True),
        lax.all_gather(down_weight, "dp", axis=0, tiled=True),
    )
    gate_pre = jnp.einsum(
        "erd,def->erf", expert_rows, full_gate, preferred_element_type=jnp.float32
    )
    up_pre = jnp.einsum("erd,def->erf", expert_rows, full_up, preferred_element_type=jnp.float32)
    sigma = jax.nn.sigmoid(gate_pre)
    active = gate_pre * sigma
    hidden = (active * up_pre).astype(jnp.bfloat16)
    expert_out = jnp.einsum(
        "erf,def->erd", hidden, full_down, preferred_element_type=jnp.float32
    ).astype(jnp.bfloat16)
    returned = to_sources(expert_out)
    flat_index = local_index.reshape(-1)
    combined = (
        jnp.zeros((tokens.shape[0], model_width), jnp.float32)
        .at[flat_index]
        .add((slot_weight[:, :, None] * returned.astype(jnp.float32)).reshape(-1, model_width))
    )
    out_grad = combined - target.astype(jnp.float32)
    slot_grad = (slot_weight[:, :, None] * out_grad[local_index]).astype(jnp.bfloat16)
    owner_grad = to_owners(slot_grad)
    hidden_grad = jnp.einsum(
        "erd,def->erf", owner_grad, full_down, preferred_element_type=jnp.float32
    )
    gate_grad = (hidden_grad * up_pre * sigma * (1.0 + gate_pre * (1.0 - sigma))).astype(
        jnp.bfloat16
    )
    up_grad = (hidden_grad * active).astype(jnp.bfloat16)
    row_grad = (
        jnp.einsum("erf,def->erd", gate_grad, full_gate, preferred_element_type=jnp.float32)
        + jnp.einsum("erf,def->erd", up_grad, full_up, preferred_element_type=jnp.float32)
    ).astype(jnp.bfloat16)
    came_back = to_sources(row_grad)
    token_grad = (
        jnp.zeros((tokens.shape[0], model_width), jnp.float32)
        .at[flat_index]
        .add(came_back.astype(jnp.float32).reshape(-1, model_width))
        .astype(jnp.bfloat16)
    )
    factor = (groups * sources * per_source) ** (-0.5)
    rows_every, grad_every = (
        lax.all_to_all(expert_rows, "dp", split_axis=2, concat_axis=1, tiled=True),
        lax.all_to_all(owner_grad, "dp", split_axis=2, concat_axis=1, tiled=True),
    )
    hidden_piece = lax.all_gather(hidden, "dp", axis=1, tiled=True)
    gate_piece = lax.all_gather(gate_grad, "dp", axis=1, tiled=True)
    up_piece = lax.all_gather(up_grad, "dp", axis=1, tiled=True)
    gate_sum = jnp.einsum(
        "erd,erf->def", rows_every, gate_piece, preferred_element_type=jnp.float32
    )
    up_sum = jnp.einsum("erd,erf->def", rows_every, up_piece, preferred_element_type=jnp.float32)
    down_sum = jnp.einsum(
        "erd,erf->def", grad_every, hidden_piece, preferred_element_type=jnp.float32
    )
    gate_gradient = gate_sum * factor
    up_gradient = up_sum * factor
    down_gradient = down_sum * factor
    return (token_grad, gate_gradient, up_gradient, down_gradient)


def solution(mesh):
    return jax.shard_map(
        on_device,
        mesh=mesh,
        in_specs=(
            P(("dp", "expert"), None),
            P(("dp", "expert"), None),
            P("dp", None, "expert", None),
            P("dp", None, "expert"),
            P("dp", None, "expert", None),
            P("dp", "expert", None),
            P("dp", "expert", None),
            P("dp", "expert", None),
        ),
        out_specs=(
            P(("dp", "expert"), None),
            P("dp", "expert", None),
            P("dp", "expert", None),
            P("dp", "expert", None),
        ),
        check_vma=False,
    )
```

profile of v0, /device:TPU:0, one launch (start us, length us, event | category | flops | bytes accessed | tf_op | source)
XLA Modules:
  0.0 305.2 jit_solution(9919206521907058066)
XLA Ops:
  11.8 5.2 %all-to-all-start = ((bf16[4,16,2048]{2,1,0:T(8,128)(2,1)}), bf16[4,16,2048]{2,1,0:T(8,128)(2,1)S(1)}, u32[]{:S(2)}, u32[]{:S(2)}) async-start(bf16[4,16,2048]{2,1,0:T(8,128)(2,1)} %broadcast_multiply_fusion), calls=%async_computation | async-start | bytes 524288 | tf_op jit(solution)/shard_map/all_to_all | solution.py:8
  18.3 4.1 %all-to-all-done = bf16[4,16,2048]{2,1,0:T(8,128)(2,1)S(1)} async-done(((bf16[4,16,2048]{2,1,0:T(8,128)(2,1)}), bf16[4,16,2048]{2,1,0:T(8,128)(2,1)S(1)}, u32[]{:S(2)}, u32[]{:S(2)}) %all-to-all-start) | async-done | bytes 262176 | tf_op jit(solution)/shard_map/all_to_all | solution.py:8
  24.9 13.3 %reduce.10 = bf16[2048,64]{1,0:T(8,128)(2,1)} reduce(bf16[2048,1,64]{2,1,0:T(2,128)(2,1)} %bitcast.114, bf16[]{:T(256)} %broadcast.134), dimensions={1}, to_apply=%bitcast.86.reduce_sub_computation | reduce | bytes 524290
  40.3 4.9 %all-to-all-start.4 = ((bf16[8,2,8192]{2,1,0:T(2,128)(2,1)}), bf16[8,2,8192]{2,1,0:T(2,128)(2,1)}, u32[]{:S(2)}, u32[]{:S(2)}) async-start(bf16[8,2,8192]{2,1,0:T(2,128)(2,1)} %reshape.301), calls=%async_computation.4 | async-start | bytes 524288 | tf_op jit(solution)/shard_map/all_to_all | solution.py:73
  46.6 8.4 %all-to-all-done.4 = bf16[8,2,8192]{2,1,0:T(2,128)(2,1)} async-done(((bf16[8,2,8192]{2,1,0:T(2,128)(2,1)}), bf16[8,2,8192]{2,1,0:T(2,128)(2,1)}, u32[]{:S(2)}, u32[]{:S(2)}) %all-to-all-start.4) | async-done | bytes 262176 | tf_op jit(solution)/shard_map/all_to_all | solution.py:73
  55.0 3.4 %reshape.302 = bf16[2048,1,64]{2,1,0:T(2,128)(2,1)} reshape(bf16[8,2,8192]{2,1,0:T(2,128)(2,1)} %all-to-all-done.4) | data formatting | bytes 524288
  58.4 3.4 %copy.41 = bf16[1,64,2048]{2,1,0:T(8,128)(2,1)} copy(bf16[1,64,2048]{1,0,2:T(2,128)(2,1)} %bitcast.112) | data formatting | bytes 524288 | tf_op jit(solution)/shard_map/all_to_all | solution.py:73
  63.5 3.2 %fusion.10 = f32[64,768]{1,0:T(8,128)} fusion(bf16[64,2048]{1,0:T(8,128)(2,1)S(1)} %bitcast.117, bf16[2048,1,768]{2,0,1:T(8,128)(2,1)} %all-gather.7.cloned.1.call-done), kind=kOutput, calls=%fused_computation.15 | convolution fusion | flops 201326592 | bytes 3604480 | tf_op jit(solution)/shard_map/erd,def->erf/dot_general | solution.py:33
  66.8 24.2 %all-gather.9.cloned.1.call-done = bf16[2048,1,768]{2,0,1:T(8,128)(2,1)} async-done(((bf16[256,1,768]{2,0,1:T(8,128)(2,1)}), bf16[2048,1,768]{2,0,1:T(8,128)(2,1)}) %all-gather.9.cloned.1.call-update) | async-done | bytes 3145744 | tf_op jit(solution)/shard_map/all_gather | solution.py:30
  90.9 3.2 %multiply_convert_fusion.3 = (bf16[64,768]{1,0:T(8,128)(2,1)S(1)}, f32[64,768]{1,0:T(8,128)}) fusion(f32[64,768]{1,0:T(8,128)} %fusion.10, bf16[64,2048]{1,0:T(8,128)(2,1)S(1)} %bitcast.118, bf16[2048,1,768]{2,0,1:T(8,128)(2,1)} %all-gather.9.cloned.1.call-done), kind=kOutput, calls=%fused_computation.44 | convolution fusion | flops 201621504 | bytes 3899392 | tf_op jit(solution)/shard_map/erd,def->erf/dot_general | solution.py:36
  94.1 35.6 %all-gather.11.cloned.1.call-done = bf16[2048,1,768]{2,0,1:T(8,128)(2,1)} async-done(((bf16[256,1,768]{2,0,1:T(8,128)(2,1)}), bf16[2048,1,768]{2,0,1:T(8,128)(2,1)}) %all-gather.11.cloned.1.call-update) | async-done | bytes 3145744 | tf_op jit(solution)/shard_map/all_gather | solution.py:31
  133.9 3.8 %reduce.8 = bf16[64,2048]{1,0:T(8,128)(2,1)} reduce(bf16[64,1,2048]{2,1,0:T(2,128)(2,1)} %bitcast.123, bf16[]{:T(256)} %broadcast.134), dimensions={1}, to_apply=%bitcast.109.reduce_sub_computation | reduce | bytes 524290
  139.5 4.2 %all-to-all-start.1 = ((bf16[4,2,16384]{2,1,0:T(2,128)(2,1)}), bf16[4,2,16384]{2,1,0:T(2,128)(2,1)}, u32[]{:S(2)}, u32[]{:S(2)}) async-start(bf16[4,2,16384]{2,1,0:T(2,128)(2,1)} %reshape.297), calls=%async_computation.1 | async-start | bytes 524288 | tf_op jit(solution)/shard_map/all_to_all | solution.py:12
  143.8 5.8 %all-to-all-done.1 = bf16[4,2,16384]{2,1,0:T(2,128)(2,1)} async-done(((bf16[4,2,16384]{2,1,0:T(2,128)(2,1)}), bf16[4,2,16384]{2,1,0:T(2,128)(2,1)}, u32[]{:S(2)}, u32[]{:S(2)}) %all-to-all-start.1) | async-done | bytes 262176 | tf_op jit(solution)/shard_map/all_to_all | solution.py:12
  151.5 5.1 %scatter_custom_fusion = f32[768,2048]{1,0:T(8,128)} fusion(s32[64]{0:T(128)S(1)} %fusion.41, f32[]{:T(128)} %constant.5.clone.1, bf16[1,64,2048]{2,0,1:T(2,128)(2,1)} %bitcast.122, f32[64]{0:T(128)S(1)} %broadcast_select_fusion.1), kind=kCustom, calls=%fused_computation.19 | custom fusion | flops 393216 | bytes 6554116 | tf_op jit(solution)/shard_map/scatter-add | solution.py:48
  156.6 7.9 %convert_subtract_fusion = f32[768,2048]{1,0:T(8,128)} fusion(f32[768,2048]{1,0:T(8,128)} %scatter_custom_fusion, bf16[768,2048]{1,0:T(8,128)(2,1)} %param.9), kind=kLoop, calls=%fused_computation.4 | loop fusion | flops 3145728 | bytes 15728640 | tf_op jit(solution)/shard_map/sub | solution.py:50
  164.4 4.6 %gather_fusion.1 = f32[64,2048]{1,0:T(8,128)} fusion(f32[768,2048]{1,0:T(8,128)} %convert_subtract_fusion, s32[1024]{0:T(1024)S(1)} %pad_clamp_fusion), kind=kCustom, calls=%fused_computation.1 | custom fusion | bytes 1048832 | tf_op jit(solution)/shard_map/gather | solution.py:51
  170.8 4.1 %all-to-all-start.2 = ((bf16[4,16,2048]{2,1,0:T(8,128)(2,1)}), bf16[4,16,2048]{2,1,0:T(8,128)(2,1)}, u32[]{:S(2)}, u32[]{:S(2)}) async-start(bf16[4,16,2048]{2,1,0:T(8,128)(2,1)} %multiply_convert_fusion), calls=%async_computation.2 | async-start | bytes 524288 | tf_op jit(solution)/shard_map/all_to_all | solution.py:8
  174.9 16.5 %all-gather.2 = bf16[512,768]{1,0:T(8,128)(2,1)} all-gather(bf16[64,768]{1,0:T(8,128)(2,1)S(1)} %get-tuple-element.28), channel_id=4, replica_groups=mesh['dp'=8,'expert'=4] {'dp'}, dimensions={0}, use_global_device_ids=true | all-gather | bytes 884736 | tf_op jit(solution)/shard_map/all_gather | solution.py:76
  197.7 3.8 %reduce.9 = bf16[64,2048]{1,0:T(8,128)(2,1)} reduce(bf16[64,1,2048]{2,1,0:T(2,128)(2,1)} %bitcast.124, bf16[]{:T(256)} %broadcast.134), dimensions={1}, to_apply=%bitcast.108.reduce_sub_computation | reduce | bytes 524290
  203.4 4.2 %all-to-all-start.3 = ((bf16[4,2,16384]{2,1,0:T(2,128)(2,1)}), bf16[4,2,16384]{2,1,0:T(2,128)(2,1)}, u32[]{:S(2)}, u32[]{:S(2)}) async-start(bf16[4,2,16384]{2,1,0:T(2,128)(2,1)} %reshape.299), calls=%async_computation.3 | async-start | bytes 524288 | tf_op jit(solution)/shard_map/all_to_all | solution.py:12
  207.6 16.5 %all-gather = bf16[512,768]{1,0:T(8,128)(2,1)S(1)} all-gather(bf16[64,768]{1,0:T(8,128)(2,1)} %copy-done.4), channel_id=2, replica_groups=mesh['dp'=8,'expert'=4] {'dp'}, dimensions={0}, use_global_device_ids=true | all-gather | bytes 884736 | tf_op jit(solution)/shard_map/all_gather | solution.py:77
  225.4 3.0 copy.46
  228.4 3.4 %copy.43 = bf16[1,64,2048]{1,0,2:T(2,128)(2,1)} copy(bf16[1,64,2048]{2,1,0:T(8,128)(2,1)} %bitcast.22) | data formatting | bytes 524288 | tf_op jit(solution)/shard_map/all_to_all | solution.py:8
  231.8 13.3 %reduce.11 = bf16[2048,64]{1,0:T(8,128)(2,1)} reduce(bf16[2048,1,64]{2,1,0:T(2,128)(2,1)} %bitcast.115, bf16[]{:T(256)} %broadcast.134), dimensions={1}, to_apply=%bitcast.88.reduce_sub_computation | reduce | bytes 524290
  247.3 4.1 %all-to-all-start.5 = ((bf16[8,2,8192]{2,1,0:T(2,128)(2,1)}), bf16[8,2,8192]{2,1,0:T(2,128)(2,1)}, u32[]{:S(2)}, u32[]{:S(2)}) async-start(bf16[8,2,8192]{2,1,0:T(2,128)(2,1)} %reshape.303), calls=%async_computation.5 | async-start | bytes 524288 | tf_op jit(solution)/shard_map/all_to_all | solution.py:74
  251.3 19.9 %all-gather.1 = bf16[512,768]{1,0:T(8,128)(2,1)S(1)} all-gather(bf16[64,768]{1,0:T(8,128)(2,1)S(1)} %get-tuple-element.25), channel_id=3, replica_groups=mesh['dp'=8,'expert'=4] {'dp'}, dimensions={0}, use_global_device_ids=true | all-gather | bytes 884736 | tf_op jit(solution)/shard_map/all_gather | solution.py:78
  272.6 3.0 copy.47
  277.5 5.1 %scatter_custom_fusion.1 = f32[768,2048]{1,0:T(8,128)} fusion(s32[64]{0:T(128)S(1)} %fusion.41, f32[]{:T(128)} %constant.5.clone.1, bf16[1,64,2048]{2,0,1:T(2,128)(2,1)} %bitcast.125), kind=kCustom, calls=%fused_computation.17 | custom fusion | flops 262144 | bytes 6553604 | tf_op jit(solution)/shard_map/scatter-add | solution.py:68
  282.5 4.9 %convert_element_type.75 = bf16[768,2048]{1,0:T(8,128)(2,1)} convert(f32[768,2048]{1,0:T(8,128)} %scatter_custom_fusion.1) | non-fusion elementwise | flops 1572864 | bytes 9437184 | tf_op jit(solution)/shard_map/convert_element_type | solution.py:69
  287.5 3.4 %reshape.304 = bf16[2048,1,64]{2,1,0:T(2,128)(2,1)} reshape(bf16[8,2,8192]{2,1,0:T(2,128)(2,1)} %all-to-all-done.5) | data formatting | bytes 524288
  295.7 3.0 copy.48
  (67 shorter events, 43.0 us)
Async XLA Ops:
  7.2 3.0 copy-start
  7.2 10.4 %copy-start.5 = (s32[1,4,1,16]{3,2,1,0:T(1,128)S(1)}, s32[1,4,1,16]{3,2,1,0:T(1,128)}, u32[]{:S(2)}) copy-start(s32[1,4,1,16]{3,2,1,0:T(1,128)} %param.10) | copy-start | bytes 772
  7.2 3.8 %copy-start.7 = (s32[1,4,1]{1,2,0:T(1,128)S(1)}, s32[1,4,1]{1,2,0:T(1,128)}, u32[]{:S(2)}) copy-start(s32[1,4,1]{1,2,0:T(1,128)} %param.11) | copy-start | bytes 52
  7.2 56.3 %all-gather.7.cloned.1.call-start = ((), (), s32[]{:S(2)}) async-start(), calls=%async_computation.6 | async-start | bytes 3538944 | tf_op jit(solution)/shard_map/all_gather | solution.py:29
  7.9 83.0 %all-gather.9.cloned.1.call-start = ((), (), s32[]{:S(2)}) async-start(), calls=%async_computation.7 | async-start | bytes 3538944 | tf_op jit(solution)/shard_map/all_gather | solution.py:30
  8.7 121.0 %all-gather.11.cloned.1.call-start = ((), (), s32[]{:S(2)}) async-start(), calls=%async_computation.8 | async-start | bytes 3538944 | tf_op jit(solution)/shard_map/all_gather | solution.py:31
  10.9 34.9 %copy-start.6 = (f32[1,4,1,16]{3,2,1,0:T(1,128)S(1)}, f32[1,4,1,16]{3,2,1,0:T(1,128)}, u32[]{:S(2)}) copy-start(f32[1,4,1,16]{3,2,1,0:T(1,128)} %param.12) | copy-start | bytes 772
  11.8 10.6 %all-to-all-start = ((bf16[4,16,2048]{2,1,0:T(8,128)(2,1)}), bf16[4,16,2048]{2,1,0:T(8,128)(2,1)S(1)}, u32[]{:S(2)}, u32[]{:S(2)}) async-start(bf16[4,16,2048]{2,1,0:T(8,128)(2,1)} %broadcast_multiply_fusion), calls=%async_computation | async-start | bytes 524288 | tf_op jit(solution)/shard_map/all_to_all | solution.py:8
  40.3 14.7 %all-to-all-start.4 = ((bf16[8,2,8192]{2,1,0:T(2,128)(2,1)}), bf16[8,2,8192]{2,1,0:T(2,128)(2,1)}, u32[]{:S(2)}, u32[]{:S(2)}) async-start(bf16[8,2,8192]{2,1,0:T(2,128)(2,1)} %reshape.301), calls=%async_computation.4 | async-start | bytes 524288 | tf_op jit(solution)/shard_map/all_to_all | solution.py:73
  94.1 49.6 %copy-start.3 = (bf16[8,8,8,256]{3,2,1,0:T(8,128)(2,1)S(1)}, bf16[8,8,8,256]{3,2,1,0:T(8,128)(2,1)}, u32[]{:S(2)}) copy-start(bf16[8,8,8,256]{3,2,1,0:T(8,128)(2,1)} %copy.49) | copy-start | bytes 786436
  139.5 10.2 %all-to-all-start.1 = ((bf16[4,2,16384]{2,1,0:T(2,128)(2,1)}), bf16[4,2,16384]{2,1,0:T(2,128)(2,1)}, u32[]{:S(2)}, u32[]{:S(2)}) async-start(bf16[4,2,16384]{2,1,0:T(2,128)(2,1)} %reshape.297), calls=%async_computation.1 | async-start | bytes 524288 | tf_op jit(solution)/shard_map/all_to_all | solution.py:12
  170.8 20.5 %all-to-all-start.2 = ((bf16[4,16,2048]{2,1,0:T(8,128)(2,1)}), bf16[4,16,2048]{2,1,0:T(8,128)(2,1)}, u32[]{:S(2)}, u32[]{:S(2)}) async-start(bf16[4,16,2048]{2,1,0:T(8,128)(2,1)} %multiply_convert_fusion), calls=%async_computation.2 | async-start | bytes 524288 | tf_op jit(solution)/shard_map/all_to_all | solution.py:8
  191.4 3.0 copy-start.2
  191.4 4.1 %copy-start.1 = (bf16[2048,1,768]{2,0,1:T(8,128)(2,1)S(1)}, bf16[2048,1,768]{2,0,1:T(8,128)(2,1)}, u32[]{:S(2)}) copy-start(bf16[2048,1,768]{2,0,1:T(8,128)(2,1)} %all-gather.7.cloned.1.call-done) | copy-start | bytes 9437188
  194.2 2.3 copy-start.4
  203.4 43.9 %all-to-all-start.3 = ((bf16[4,2,16384]{2,1,0:T(2,128)(2,1)}), bf16[4,2,16384]{2,1,0:T(2,128)(2,1)}, u32[]{:S(2)}, u32[]{:S(2)}) async-start(bf16[4,2,16384]{2,1,0:T(2,128)(2,1)} %reshape.299), calls=%async_computation.3 | async-start | bytes 524288 | tf_op jit(solution)/shard_map/all_to_all | solution.py:12
  247.3 40.2 %all-to-all-start.5 = ((bf16[8,2,8192]{2,1,0:T(2,128)(2,1)}), bf16[8,2,8192]{2,1,0:T(2,128)(2,1)}, u32[]{:S(2)}, u32[]{:S(2)}) async-start(bf16[8,2,8192]{2,1,0:T(2,128)(2,1)} %reshape.303), calls=%async_computation.5 | async-start | bytes 524288 | tf_op jit(solution)/shard_map/all_to_all | solution.py:74
Sparse Core Ops, SparseCore 0:
  9.6 40.9 all-gather.6
  52.3 38.6 all-gather.8
  92.6 37.1 all-gather.10
where the time goes:
time: 307 us; the launch traced here: 305 us
  waiting for transfers between devices  80.1 us (26%)
  other arithmetic  62 us (20%)
  blocking collectives  52.9 us (17%)
  local copies, waits for them, and re-layouts  50.3 us (16%)
  starting transfers between devices  26.7 us (9%)
  matrix products  19.3 us (6%)
  between operations  13.9 us (5%)
    all_gather x1, waiting for transfers between devices, on_device(): lax.all_gather(down_weight, 'dp', axis=0, tiled=True)  35.6 us
    unnamed x6, other arithmetic  35.6 us
    unnamed x32, local copies, waits for them, and re-layouts  31.1 us
    all_gather x1, waiting for transfers between devices, on_device(): lax.all_gather(up_weight, 'dp', axis=0, tiled=True)  24.2 us
    all_gather x1, blocking collectives, on_device(): up_piece = lax.all_gather(up_grad, 'dp', axis=1, tiled=True)  19.9 us
    all_gather x1, blocking collectives, on_device(): gate_piece = lax.all_gather(gate_grad, 'dp', axis=1, tiled=True)  16.5 us
    all_gather x1, blocking collectives, on_device(): hidden_piece = lax.all_gather(hidden, 'dp', axis=1, tiled=True)  16.5 us
    all_to_all x2, starting transfers between devices, to_owners(): lax.all_to_all(block, 'expert', split_axis=0, concat_axis=1, tiled=True)  9.24 us
  transfers between devices with their start and end apart: 9, of which 5 were waited for; matrix products, arithmetic and copies ran while one was open for 25% of the time, Pallas kernels for 0%

commit v1 on v0

--- a/solution.py
+++ b/solution.py
@@ -74,8 +74,11 @@
         lax.all_to_all(owner_grad, "dp", split_axis=2, concat_axis=1, tiled=True),
     )
     hidden_piece = lax.all_gather(hidden, "dp", axis=1, tiled=True)
-    gate_piece = lax.all_gather(gate_grad, "dp", axis=1, tiled=True)
-    up_piece = lax.all_gather(up_grad, "dp", axis=1, tiled=True)
+    gate_piece, up_piece = jnp.split(
+        lax.all_gather(jnp.concatenate([gate_grad, up_grad], axis=0), "dp", axis=1, tiled=True),
+        [gate_grad.shape[0]],
+        axis=0,
+    )
     gate_sum = jnp.einsum(
         "erd,erf->def", rows_every, gate_piece, preferred_element_type=jnp.float32
     )

time: 307 us -> 311 us (1.013)
  waiting for transfers between devices: 80.1 us -> 110 us
  blocking collectives: 52.9 us -> 26.8 us
  matrix products: 19.3 us -> 23.5 us
  starting transfers between devices: 26.7 us -> 22.7 us
    all_gather x2 -> x0, blocking collectives: 36.4 us -> none  [the longest x1 19.9 us: on_device(): up_piece = lax.all_gather(up_grad, 'dp', axis=1, tiled=True)]
    all_gather x1, waiting for transfers between devices: 0.01 us -> 28.2 us  [on_device(): lax.all_gather(gate_weight, 'dp', axis=0, tiled=True)]
    all_gather x1, waiting for transfers between devices: 24.2 us -> 35.6 us  [on_device(): lax.all_gather(up_weight, 'dp', axis=0, tiled=True)]
    all_to_all x1, waiting for transfers between devices: 8.38 us -> 0.01 us  [on_device(): lax.all_to_all(expert_rows, 'dp', split_axis=2, concat_axis=1, tiled=True)]
    all_to_all x0 -> x1, blocking collectives: none -> 8.11 us  [to_owners(): lax.all_to_all(block, 'expert', split_axis=0, concat_axis=1, tiled=True)]
    all_to_all x2 -> x1, starting transfers between devices: 9.24 us -> 5.19 us  [to_owners(): lax.all_to_all(block, 'expert', split_axis=0, concat_axis=1, tiled=True)]
    unnamed x32 -> x38, local copies, waits for them, and re-layouts: 31.1 us -> 30.7 us
  transfers between devices with their start and end apart: 9 -> 9, of which waited for: 5 -> 5; matrix products, arithmetic and copies ran while one was open for 25% -> 29% of each run, Pallas kernels for 0% -> 0%
where the time goes in v1:
time: 311 us; the launch traced here: 309 us
  waiting for transfers between devices  110 us (35%)
  other arithmetic  61.8 us (20%)
  local copies, waits for them, and re-layouts  50.1 us (16%)
  blocking collectives  26.8 us (9%)
  matrix products  23.5 us (8%)
  starting transfers between devices  22.7 us (7%)
  between operations  14 us (5%)
    all_gather x1, waiting for transfers between devices, on_device(): lax.all_gather(down_weight, 'dp', axis=0, tiled=True)  35.6 us
    all_gather x1, waiting for transfers between devices, on_device(): lax.all_gather(up_weight, 'dp', axis=0, tiled=True)  35.6 us
    unnamed x6, other arithmetic  35.5 us
    unnamed x38, local copies, waits for them, and re-layouts  30.7 us
    all_gather x1, waiting for transfers between devices, on_device(): lax.all_gather(gate_weight, 'dp', axis=0, tiled=True)  28.2 us
    all_gather x1, blocking collectives, on_device(): hidden_piece = lax.all_gather(hidden, 'dp', axis=1, tiled=True)  18.7 us
    all_to_all x2, starting transfers between devices, to_sources(): lax.all_to_all(block, 'expert', split_axis=1, concat_axis=0, tiled=True)  8.33 us
    all_to_all x1, blocking collectives, to_owners(): lax.all_to_all(block, 'expert', split_axis=0, concat_axis=1, tiled=True)  8.11 us
  transfers between devices with their start and end apart: 9, of which 5 were waited for; matrix products, arithmetic and copies ran while one was open for 29% of the time, Pallas kernels for 0%

profile of v1, /device:TPU:0, one launch (start us, length us, event | category | flops | bytes accessed | tf_op | source)
XLA Modules:
  0.0 309.1 jit_solution(15900074984230849162)
XLA Ops:
  11.8 5.2 %all-to-all-start = ((bf16[4,16,2048]{2,1,0:T(8,128)(2,1)}), bf16[4,16,2048]{2,1,0:T(8,128)(2,1)S(1)}, u32[]{:S(2)}, u32[]{:S(2)}) async-start(bf16[4,16,2048]{2,1,0:T(8,128)(2,1)} %broadcast_multiply_fusion), calls=%async_computation | async-start | bytes 524288 | tf_op jit(solution)/shard_map/all_to_all | solution.py:8
  19.7 2.7 all-to-all-done
  22.4 28.2 %all-gather.6.cloned.1.call-done = bf16[2048,1,768]{2,0,1:T(8,128)(2,1)} async-done(((bf16[256,1,768]{2,0,1:T(8,128)(2,1)}), bf16[2048,1,768]{2,0,1:T(8,128)(2,1)}) %all-gather.6.cloned.1.call-update) | async-done | bytes 3145744 | tf_op jit(solution)/shard_map/all_gather | solution.py:29
  50.6 3.2 %fusion.10 = f32[64,768]{1,0:T(8,128)} fusion(bf16[64,2048]{1,0:T(8,128)(2,1)S(1)} %bitcast.122, bf16[2048,1,768]{2,0,1:T(8,128)(2,1)} %all-gather.6.cloned.1.call-done), kind=kOutput, calls=%fused_computation.15 | convolution fusion | flops 201326592 | bytes 3604480 | tf_op jit(solution)/shard_map/erd,def->erf/dot_general | solution.py:33
  53.8 35.6 %all-gather.8.cloned.1.call-done = bf16[2048,1,768]{2,0,1:T(8,128)(2,1)} async-done(((bf16[256,1,768]{2,0,1:T(8,128)(2,1)}), bf16[2048,1,768]{2,0,1:T(8,128)(2,1)}) %all-gather.8.cloned.1.call-update) | async-done | bytes 3145744 | tf_op jit(solution)/shard_map/all_gather | solution.py:30
  89.4 3.2 %multiply_convert_fusion.3 = (bf16[64,768]{1,0:T(8,128)(2,1)S(1)}, f32[64,768]{1,0:T(8,128)}) fusion(f32[64,768]{1,0:T(8,128)} %fusion.10, bf16[64,2048]{1,0:T(8,128)(2,1)S(1)} %bitcast.123, bf16[2048,1,768]{2,0,1:T(8,128)(2,1)} %all-gather.8.cloned.1.call-done), kind=kOutput, calls=%fused_computation.47 | convolution fusion | flops 201621504 | bytes 3899392 | tf_op jit(solution)/shard_map/erd,def->erf/dot_general | solution.py:36
  92.6 35.6 %all-gather.10.cloned.1.call-done = bf16[2048,1,768]{2,0,1:T(8,128)(2,1)} async-done(((bf16[256,1,768]{2,0,1:T(8,128)(2,1)}), bf16[2048,1,768]{2,0,1:T(8,128)(2,1)}) %all-gather.10.cloned.1.call-update) | async-done | bytes 3145744 | tf_op jit(solution)/shard_map/all_gather | solution.py:31
  128.2 3.0 fusion.25
  132.9 3.8 %reduce.8 = bf16[64,2048]{1,0:T(8,128)(2,1)} reduce(bf16[64,1,2048]{2,1,0:T(2,128)(2,1)} %bitcast.129, bf16[]{:T(256)} %broadcast.134), dimensions={1}, to_apply=%bitcast.115.reduce_sub_computation | reduce | bytes 524290
  138.5 4.1 %all-to-all-start.1 = ((bf16[4,2,16384]{2,1,0:T(2,128)(2,1)}), bf16[4,2,16384]{2,1,0:T(2,128)(2,1)}, u32[]{:S(2)}, u32[]{:S(2)}) async-start(bf16[4,2,16384]{2,1,0:T(2,128)(2,1)} %reshape.293), calls=%async_computation.1 | async-start | bytes 524288 | tf_op jit(solution)/shard_map/all_to_all | solution.py:12
  142.6 6.0 %all-to-all-done.1 = bf16[4,2,16384]{2,1,0:T(2,128)(2,1)} async-done(((bf16[4,2,16384]{2,1,0:T(2,128)(2,1)}), bf16[4,2,16384]{2,1,0:T(2,128)(2,1)}, u32[]{:S(2)}, u32[]{:S(2)}) %all-to-all-start.1) | async-done | bytes 262176 | tf_op jit(solution)/shard_map/all_to_all | solution.py:12
  150.5 5.0 %scatter_custom_fusion = f32[768,2048]{1,0:T(8,128)} fusion(s32[64]{0:T(128)S(1)} %fusion.41, f32[]{:T(128)} %constant.5.clone.1, bf16[1,64,2048]{2,0,1:T(2,128)(2,1)} %bitcast.128, f32[64]{0:T(128)S(1)} %broadcast_select_fusion.1), kind=kCustom, calls=%fused_computation.19 | custom fusion | flops 393216 | bytes 6554116 | tf_op jit(solution)/shard_map/scatter-add | solution.py:48
  155.6 7.8 %convert_subtract_fusion = f32[768,2048]{1,0:T(8,128)} fusion(f32[768,2048]{1,0:T(8,128)} %scatter_custom_fusion, bf16[768,2048]{1,0:T(8,128)(2,1)} %param.9), kind=kLoop, calls=%fused_computation.4 | loop fusion | flops 3145728 | bytes 15728640 | tf_op jit(solution)/shard_map/sub | solution.py:50
  163.4 4.6 %gather_fusion.1 = f32[64,2048]{1,0:T(8,128)} fusion(f32[768,2048]{1,0:T(8,128)} %convert_subtract_fusion, s32[1024]{0:T(1024)S(1)} %pad_clamp_fusion), kind=kCustom, calls=%fused_computation.1 | custom fusion | bytes 1048832 | tf_op jit(solution)/shard_map/gather | solution.py:51
  169.1 8.1 %all_to_all.72 = bf16[4,16,2048]{2,1,0:T(8,128)(2,1)S(1)} all-to-all(bf16[4,16,2048]{2,1,0:T(8,128)(2,1)S(1)} %multiply_convert_fusion), channel_id=1, replica_groups=mesh['dp'=8,'expert'=4] {'expert'}, dimensions={0} | all-to-all | bytes 524288 | tf_op jit(solution)/shard_map/all_to_all | solution.py:8
  177.9 2.7 multiply_convert_fusion.2
  183.9 13.3 %reduce.10 = bf16[2048,64]{1,0:T(8,128)(2,1)} reduce(bf16[2048,1,64]{2,1,0:T(2,128)(2,1)} %bitcast.121, bf16[]{:T(256)} %broadcast.134), dimensions={1}, to_apply=%bitcast.94.reduce_sub_computation | reduce | bytes 524290
  199.4 4.0 %all-to-all-start.4 = ((bf16[8,2,8192]{2,1,0:T(2,128)(2,1)}), bf16[8,2,8192]{2,1,0:T(2,128)(2,1)}, u32[]{:S(2)}, u32[]{:S(2)}) async-start(bf16[8,2,8192]{2,1,0:T(2,128)(2,1)} %reshape.297), calls=%async_computation.4 | async-start | bytes 524288 | tf_op jit(solution)/shard_map/all_to_all | solution.py:73
  203.5 3.2 %fusion.4 = f32[64,2048]{1,0:T(8,128)S(1)} fusion(bf16[64,768]{1,0:T(8,128)(2,1)} %copy-done.6, bf16[2048,1,768]{2,0,1:T(8,128)(2,1)} %all-gather.8.cloned.1.call-done), kind=kOutput, calls=%fused_computation.9 | convolution fusion | flops 201326592 | bytes 3768320 | tf_op jit(solution)/shard_map/erf,def->erd/dot_general | solution.py:62
  208.9 3.8 %reduce.9 = bf16[64,2048]{1,0:T(8,128)(2,1)} reduce(bf16[64,1,2048]{2,1,0:T(2,128)(2,1)} %bitcast.130, bf16[]{:T(256)} %broadcast.134), dimensions={1}, to_apply=%bitcast.114.reduce_sub_computation | reduce | bytes 524290
  214.5 4.3 %all-to-all-start.3 = ((bf16[4,2,16384]{2,1,0:T(2,128)(2,1)}), bf16[4,2,16384]{2,1,0:T(2,128)(2,1)}, u32[]{:S(2)}, u32[]{:S(2)}) async-start(bf16[4,2,16384]{2,1,0:T(2,128)(2,1)} %reshape.295), calls=%async_computation.3 | async-start | bytes 524288 | tf_op jit(solution)/shard_map/all_to_all | solution.py:12
  218.8 3.4 %reshape.298 = bf16[2048,1,64]{2,1,0:T(2,128)(2,1)} reshape(bf16[8,2,8192]{2,1,0:T(2,128)(2,1)} %all-to-all-done.4) | data formatting | bytes 524288
  222.2 3.4 %copy.41 = bf16[1,64,2048]{2,1,0:T(8,128)(2,1)} copy(bf16[1,64,2048]{1,0,2:T(2,128)(2,1)} %bitcast.118) | data formatting | bytes 524288 | tf_op jit(solution)/shard_map/all_to_all | solution.py:73
  229.3 13.3 %reduce.11 = bf16[2048,64]{1,0:T(8,128)(2,1)} reduce(bf16[2048,1,64]{2,1,0:T(2,128)(2,1)} %bitcast.120, bf16[]{:T(256)} %broadcast.134), dimensions={1}, to_apply=%bitcast.96.reduce_sub_computation | reduce | bytes 524290
  244.7 5.0 %all-to-all-start.5 = ((bf16[8,2,8192]{2,1,0:T(2,128)(2,1)}), bf16[8,2,8192]{2,1,0:T(2,128)(2,1)S(1)}, u32[]{:S(2)}, u32[]{:S(2)}) async-start(bf16[8,2,8192]{2,1,0:T(2,128)(2,1)} %reshape.299), calls=%async_computation.5 | async-start | bytes 524288 | tf_op jit(solution)/shard_map/all_to_all | solution.py:74
  251.4 18.7 %all-gather = bf16[512,768]{1,0:T(8,128)(2,1)} all-gather(bf16[64,768]{1,0:T(8,128)(2,1)S(1)} %get-tuple-element.28), channel_id=2, replica_groups=mesh['dp'=8,'expert'=4] {'dp'}, dimensions={0}, use_global_device_ids=true | all-gather | bytes 884736 | tf_op jit(solution)/shard_map/all_gather | solution.py:76
  272.0 5.0 %scatter_custom_fusion.1 = f32[768,2048]{1,0:T(8,128)} fusion(s32[64]{0:T(128)S(1)} %fusion.41, f32[]{:T(128)} %constant.5.clone.1, bf16[1,64,2048]{2,0,1:T(2,128)(2,1)} %bitcast.131), kind=kCustom, calls=%fused_computation.17 | custom fusion | flops 262144 | bytes 6553604 | tf_op jit(solution)/shard_map/scatter-add | solution.py:68
  277.0 4.9 %convert_element_type.75 = bf16[768,2048]{1,0:T(8,128)(2,1)} convert(f32[768,2048]{1,0:T(8,128)} %scatter_custom_fusion.1) | non-fusion elementwise | flops 1572864 | bytes 9437184 | tf_op jit(solution)/shard_map/convert_element_type | solution.py:69
  288.7 3.0 copy.48
  294.1 3.0 copy.46
  297.2 2.4 fusion.32
  299.6 3.0 copy.47
  (74 shorter events, 42.7 us)
Async XLA Ops:
  7.2 3.0 copy-start
  7.2 10.4 %copy-start.8 = (s32[1,4,1,16]{3,2,1,0:T(1,128)S(1)}, s32[1,4,1,16]{3,2,1,0:T(1,128)}, u32[]{:S(2)}) copy-start(s32[1,4,1,16]{3,2,1,0:T(1,128)} %param.10) | copy-start | bytes 772
  7.2 3.8 %copy-start.10 = (s32[1,4,1]{1,2,0:T(1,128)S(1)}, s32[1,4,1]{1,2,0:T(1,128)}, u32[]{:S(2)}) copy-start(s32[1,4,1]{1,2,0:T(1,128)} %param.11) | copy-start | bytes 52
  7.2 11.7 %copy-start.9 = (f32[1,4,1,16]{3,2,1,0:T(1,128)S(1)}, f32[1,4,1,16]{3,2,1,0:T(1,128)}, u32[]{:S(2)}) copy-start(f32[1,4,1,16]{3,2,1,0:T(1,128)} %param.12) | copy-start | bytes 772
  7.2 43.4 %all-gather.6.cloned.1.call-start = ((), (), s32[]{:S(2)}) async-start(), calls=%async_computation.6 | async-start | bytes 3538944 | tf_op jit(solution)/shard_map/all_gather | solution.py:29
  7.9 81.5 %all-gather.8.cloned.1.call-start = ((), (), s32[]{:S(2)}) async-start(), calls=%async_computation.7 | async-start | bytes 3538944 | tf_op jit(solution)/shard_map/all_gather | solution.py:30
  8.7 119.5 %all-gather.10.cloned.1.call-start = ((), (), s32[]{:S(2)}) async-start(), calls=%async_computation.8 | async-start | bytes 3538944 | tf_op jit(solution)/shard_map/all_gather | solution.py:31
  11.8 10.6 %all-to-all-start = ((bf16[4,16,2048]{2,1,0:T(8,128)(2,1)}), bf16[4,16,2048]{2,1,0:T(8,128)(2,1)S(1)}, u32[]{:S(2)}, u32[]{:S(2)}) async-start(bf16[4,16,2048]{2,1,0:T(8,128)(2,1)} %broadcast_multiply_fusion), calls=%async_computation | async-start | bytes 524288 | tf_op jit(solution)/shard_map/all_to_all | solution.py:8
  138.5 10.2 %all-to-all-start.1 = ((bf16[4,2,16384]{2,1,0:T(2,128)(2,1)}), bf16[4,2,16384]{2,1,0:T(2,128)(2,1)}, u32[]{:S(2)}, u32[]{:S(2)}) async-start(bf16[4,2,16384]{2,1,0:T(2,128)(2,1)} %reshape.293), calls=%async_computation.1 | async-start | bytes 524288 | tf_op jit(solution)/shard_map/all_to_all | solution.py:12
  142.6 149.1 %all-gather.12.cloned.1.call-start = ((), (), s32[]{:S(2)}) async-start(), calls=%async_computation.9 | async-start | bytes 1769472 | tf_op jit(solution)/shard_map/all_gather | solution.py:78
  177.2 0.7 copy-start.2
  180.6 0.6 copy-start.4
  180.6 0.7 copy-start.6
  183.9 22.7 %copy-start.5 = (bf16[64,768]{1,0:T(8,128)(2,1)S(1)}, bf16[64,768]{1,0:T(8,128)(2,1)}, u32[]{:S(2)}) copy-start(bf16[64,768]{1,0:T(8,128)(2,1)} %copy-done.4) | copy-start | bytes 294916
  199.4 15.1 %all-to-all-start.4 = ((bf16[8,2,8192]{2,1,0:T(2,128)(2,1)}), bf16[8,2,8192]{2,1,0:T(2,128)(2,1)}, u32[]{:S(2)}, u32[]{:S(2)}) async-start(bf16[8,2,8192]{2,1,0:T(2,128)(2,1)} %reshape.297), calls=%async_computation.4 | async-start | bytes 524288 | tf_op jit(solution)/shard_map/all_to_all | solution.py:73
  203.5 3.2 %copy-start.1 = (bf16[2048,1,768]{2,0,1:T(8,128)(2,1)S(1)}, bf16[2048,1,768]{2,0,1:T(8,128)(2,1)}, u32[]{:S(2)}) copy-start(bf16[2048,1,768]{2,0,1:T(8,128)(2,1)} %all-gather.6.cloned.1.call-done) | copy-start | bytes 9437188
  207.7 19.6 %copy-start.3 = (bf16[4,16,2048]{2,1,0:T(8,128)(2,1)S(1)}, bf16[4,16,2048]{2,1,0:T(8,128)(2,1)}, u32[]{:S(2)}) copy-start(bf16[4,16,2048]{2,1,0:T(8,128)(2,1)} %copy-done.2) | copy-start | bytes 786436
  214.5 30.1 %all-to-all-start.3 = ((bf16[4,2,16384]{2,1,0:T(2,128)(2,1)}), bf16[4,2,16384]{2,1,0:T(2,128)(2,1)}, u32[]{:S(2)}, u32[]{:S(2)}) async-start(bf16[4,2,16384]{2,1,0:T(2,128)(2,1)} %reshape.295), calls=%async_computation.3 | async-start | bytes 524288 | tf_op jit(solution)/shard_map/all_to_all | solution.py:12
  244.7 37.3 %all-to-all-start.5 = ((bf16[8,2,8192]{2,1,0:T(2,128)(2,1)}), bf16[8,2,8192]{2,1,0:T(2,128)(2,1)S(1)}, u32[]{:S(2)}, u32[]{:S(2)}) async-start(bf16[8,2,8192]{2,1,0:T(2,128)(2,1)} %reshape.299), calls=%async_computation.5 | async-start | bytes 524288 | tf_op jit(solution)/shard_map/all_to_all | solution.py:74
  286.2 5.5 %copy-start.7 = (bf16[1,8,64,256]{3,2,1,0:T(8,128)(2,1)S(1)}, bf16[1,8,64,256]{3,2,1,0:T(8,128)(2,1)}, u32[]{:S(2)}) copy-start(bf16[1,8,64,256]{3,2,1,0:T(8,128)(2,1)} %copy.42) | copy-start | bytes 786436
Sparse Core Ops, SparseCore 0:
  9.7 40.9 all-gather.5
  52.3 37.1 all-gather.7
  91.1 37.1 all-gather.9
  182.1 22.7 all-gather.11
